TPU v7x, 32 devices: a whole 2x2x4 slice. The times are simulated.
32 devices in a mesh: members: 2 (over y), lat: 4 (over z), lev: 2 (over x), sub: 2 (over core).
Axes of the slice: x: 2, y: 2, z: 4, core: 2. Of those that a mesh axis runs over, the one named last changes fastest.
Arguments:
- thermal_state_grid: bfloat16 [272, 512, 1024], P(('members', 'lev', 'sub'), 'lat'), parts along dimension 0, may hold values from -6 to 6
- thermal_forcing: bfloat16 [272, 512, 1024], P(('members', 'lev', 'sub'), 'lat'), parts along dimension 0, may hold values from -6 to 6
- spherical_basis_table: bfloat16 [512, 512, 512], P(('lat', 'lev', 'sub')), may hold values from -0.25 to 0.25
- implicit_solver_matrix: bfloat16 [512, 136, 136], P(('lat', 'lev', 'sub')), may hold values from -0.5 to 0.5
- fourier_order_holder: int32 [512], replicated, may hold values from 0 to 511, as said below
Outputs:
- new_temperature: bfloat16 [272, 512, 1024], P(('members', 'lev', 'sub'), 'lat'), parts along dimension 0
There are 2 independent parts, one for each index of `members`. A program takes and returns all parts, laid end to end along the dimension named above; an argument that names none is the same for every part. Nothing has to cross between parts.
Inputs may be any that keep to these rules, and one draw needn't show every extreme that they name: fourier_order_holder is a permutation of the waves; slots 2k and 2k+1 hold waves m and 511-m for some m.
All inputs are finite; a program needn't handle non-finite values.
Results may differ from a plain program's by a relative error of at most 0.0079.
Values may be sent and summed in bfloat16 or wider, within the bound.
A program may use at most 192 MiB of HBM per device.

v0:
```python
import math
import jax
import jax.numpy as jnp
from jax import lax
from jax.sharding import PartitionSpec as P


def raw_table(fourier_order_holder, lon_count):
    meridian_position = jnp.arange(lon_count, dtype=jnp.int32)
    phases = meridian_position[:, None] * fourier_order_holder[None, :] % lon_count
    angles = phases.astype(jnp.float32) * (2.0 * math.pi / lon_count)
    factor = 1.0 / math.sqrt(lon_count)
    stacked = jnp.stack([jnp.cos(angles), -jnp.sin(angles)], axis=2)
    return stacked.reshape(lon_count, 2 * fourier_order_holder.shape[0]) * factor


def shards(
    thermal_state_grid,
    thermal_forcing,
    spherical_basis_table,
    implicit_solver_matrix,
    fourier_order_holder,
):
    layer_group_span, parallel_group_span, meridian_position = thermal_state_grid.shape
    slot_count, lat_total, wave_total = spherical_basis_table.shape
    present_state = thermal_state_grid.astype(jnp.float32)
    explicit = (
        present_state
        + 0.5 * thermal_forcing.astype(jnp.float32)
        - 0.3
        * present_state
        * present_state
        * present_state
        / (1.0 + present_state * present_state)
    ).astype(jnp.bfloat16)
    raw = raw_table(fourier_order_holder, meridian_position)
    analysis = raw.astype(jnp.bfloat16)
    weights = jnp.where(fourier_order_holder == 0, 1.0, 2.0).astype(jnp.float32)
    synthesis = (raw.T * jnp.repeat(weights, 2)[:, None]).astype(jnp.bfloat16)
    spectral = jnp.dot(
        explicit.reshape(layer_group_span * parallel_group_span, meridian_position),
        analysis,
        preferred_element_type=jnp.float32,
    )
    spectral = spectral.astype(jnp.bfloat16).reshape(
        layer_group_span, parallel_group_span, meridian_position
    )
    banded = lax.all_to_all(spectral, "lat", split_axis=2, concat_axis=1, tiled=True)
    gathered = lax.all_gather(spherical_basis_table, ("lev", "sub"), axis=0, tiled=True)
    owner_slots = gathered.shape[0]
    by_slot = banded.reshape(layer_group_span, lat_total, owner_slots, 2)
    part_spec = jnp.einsum(
        "lxsc,sxn->lscn", by_slot, gathered, preferred_element_type=jnp.float32
    ).astype(jnp.bfloat16)
    column = lax.all_to_all(part_spec, ("lev", "sub"), split_axis=1, concat_axis=0, tiled=True)
    solved = jnp.einsum(
        "skl,lscn->kscn", implicit_solver_matrix, column, preferred_element_type=jnp.float32
    )
    owner_index = lax.axis_index(("lat", "lev", "sub"))
    my_waves = lax.dynamic_slice_in_dim(fourier_order_holder, owner_index * slot_count, slot_count)
    degrees = jnp.arange(wave_total, dtype=jnp.int32)
    live_mask = degrees[None, :] >= my_waves[:, None]
    solved = jnp.where(live_mask[None, :, None, :], solved, 0.0).astype(jnp.bfloat16)
    returned = lax.all_to_all(solved, ("lev", "sub"), split_axis=0, concat_axis=1, tiled=True)
    synthesized = jnp.einsum(
        "sxn,lscn->lxsc", gathered, returned, preferred_element_type=jnp.float32
    ).astype(jnp.bfloat16)
    synthesized = synthesized.reshape(layer_group_span, lat_total, 2 * owner_slots)
    grid_spec = lax.all_to_all(synthesized, "lat", split_axis=1, concat_axis=2, tiled=True)
    result = jnp.dot(
        grid_spec.reshape(layer_group_span * parallel_group_span, meridian_position),
        synthesis,
        preferred_element_type=jnp.float32,
    )
    return result.astype(jnp.bfloat16).reshape(
        layer_group_span, parallel_group_span, meridian_position
    )


def solution(mesh):
    return jax.shard_map(
        shards,
        mesh=mesh,
        in_specs=(
            P(("members", "lev", "sub"), "lat", None),
            P(("members", "lev", "sub"), "lat", None),
            P(("lat", "lev", "sub"), None, None),
            P(("lat", "lev", "sub"), None, None),
            P(),
        ),
        out_specs=P(("members", "lev", "sub"), "lat", None),
        check_vma=False,
    )
```

profile of v0, /device:TPU:0, one launch (start us, length us, event | category | flops | bytes accessed | tf_op | source)
XLA Modules:
  0.0 1055.7 jit_solution(9948861162757677807)
XLA Ops:
  6.5 0.0 copy-start
  6.5 0.0 copy-start.3
  6.5 0.0 all-gather.2.cloned.1.call-start
  6.5 0.7 all-gather.2.cloned.1.call-update
  7.3 0.1 copy-done.3
  7.4 8.2 fusion.25
  15.6 4.4 maximum_multiply_fusion
  20.0 7.0 copy.51
  27.0 4.5 convert_element_type.68
  31.5 0.0 copy-start.2
  31.5 13.7 %fusion.5 = bf16[34,128,1024]{2,1,0:T(8,128)(2,1)S(1)} fusion(bf16[34,128,1024]{2,1,0:T(8,128)(2,1)} %param.5, bf16[34,128,1024]{2,1,0:T(8,128)(2,1)} %param.6), kind=kLoop, calls=%fused_computation.10 | loop fusion | flops 53477376 | bytes 26738688 | tf_op jit(solution)/shard_map/convert_element_type | solution.py:35
  45.2 0.0 copy-done.2
  45.2 11.6 %convolution_convert_fusion.1 = bf16[4352,1024]{1,0:T(8,128)(2,1)} fusion(bf16[4352,1024]{1,0:T(8,128)(2,1)S(1)} %bitcast.63, bf16[1024,1024]{0,1:T(8,128)(2,1)S(1)} %copy-done.2), kind=kOutput, calls=%fused_computation.16 | convolution fusion | flops 9131261952 | bytes 19922944 | tf_op jit(solution)/shard_map/dot_general | solution.py:40
  56.8 15.1 %copy.52 = bf16[34,128,1024]{1,0,2:T(8,128)(2,1)} copy(bf16[34,128,1024]{2,1,0:T(8,128)(2,1)} %bitcast.61) | data formatting | bytes 17825792 | tf_op jit(solution)/shard_map/reshape | solution.py:45
  71.9 234.5 %all_to_all.66 = bf16[34,128,1024]{1,0,2:T(8,128)(2,1)S(1)} all-to-all(bf16[34,128,1024]{1,0,2:T(8,128)(2,1)} %copy.52), channel_id=1, replica_groups=mesh['members'=2,'lat'=4,'lev'=2,'sub'=2] {'lat'}, dimensions={2} | all-to-all | bytes 17825792 | tf_op jit(solution)/shard_map/all_to_all | solution.py:48
  306.5 8.5 copy.70
  314.9 16.5 %reshape.153 = bf16[34,512,128,2]{1,0,3,2:T(8,128)(2,1)} reshape(bf16[34,4,128,256]{2,1,0,3:T(4,128)(2,1)} %copy.70) | data formatting | bytes 17825792 | tf_op jit(solution)/shard_map/reshape | solution.py:51
  331.4 73.0 %all-gather.2.cloned.1.call-done = bf16[128,512,512]{2,1,0:T(8,128)(2,1)} async-done(((bf16[32,512,512]{2,1,0:T(8,128)(2,1)}), bf16[128,512,512]{2,1,0:T(8,128)(2,1)}) %all-gather.2.cloned.1.call-update) | async-done | bytes 67108880 | tf_op jit(solution)/shard_map/all_gather | solution.py:49
  404.4 30.4 %convert_bitcast_fusion = bf16[34,128,2,512]{3,0,2,1:T(8,128)(2,1)} fusion(bf16[34,512,128,2]{1,0,3,2:T(8,128)(2,1)} %reshape.153, bf16[128,512,512]{2,1,0:T(8,128)(2,1)} %all-gather.2.cloned.1.call-done), kind=kOutput, calls=%fused_computation.14 | convolution fusion | flops 4567859200 | bytes 84934656 | tf_op jit(solution)/shard_map/lxsc,sxn->lscn/dot_general | solution.py:52
  434.8 13.8 %copy.56 = bf16[34,128,2,512]{3,2,0,1:T(2,128)(2,1)} copy(bf16[34,128,2,512]{3,0,2,1:T(8,128)(2,1)} %convert_bitcast_fusion) | data formatting | bytes 17825792 | tf_op jit(solution)/shard_map/convert_element_type | solution.py:54
  448.6 6.0 all-to-all-start.1
  454.6 0.1 dynamic_slice.3
  454.6 0.1 iota_compare_fusion
  454.7 98.6 %all-to-all-done.1 = bf16[34,128,2,512]{3,2,0,1:T(2,128)(2,1)} async-done(((bf16[34,128,2,512]{3,2,0,1:T(2,128)(2,1)}), bf16[34,128,2,512]{3,2,0,1:T(2,128)(2,1)}, u32[]{:S(2)}, u32[]{:S(2)}) %all-to-all-start.1) | async-done | bytes 8912928 | tf_op jit(solution)/shard_map/all_to_all | solution.py:55
  553.3 9.5 copy.57
  562.8 8.8 copy.58
  571.6 0.0 copy-done
  571.6 16.3 %fusion.14 = bf16[136,32,2,512]{3,0,2,1:T(8,128)(2,1)S(1)} fusion(bf16[136,32,2,512]{3,1,2,0:T(8,128)(2,1)} %bitcast.62, pred[32,512]{1,0:T(8,128)(4,1)S(1)} %iota_compare_fusion, bf16[32,136,136]{2,1,0:T(8,128)(2,1)S(1)} %copy-done), kind=kOutput, calls=%fused_computation.19 | convolution fusion | flops 1221066752 | bytes 19025920 | tf_op jit(solution)/shard_map/skl,lscn->kscn/dot_general | solution.py:56
  587.8 11.6 %copy.60 = bf16[136,32,2,512]{3,2,1,0:T(2,128)(2,1)S(1)} copy(bf16[136,32,2,512]{3,0,2,1:T(8,128)(2,1)S(1)} %fusion.14) | data formatting | bytes 17825792 | tf_op jit(solution)/shard_map/convert_element_type | solution.py:63
  599.4 103.0 %all_to_all.67 = bf16[136,32,2,512]{3,2,1,0:T(2,128)(2,1)} all-to-all(bf16[136,32,2,512]{3,2,1,0:T(2,128)(2,1)S(1)} %copy.60), channel_id=1, replica_groups=mesh['members'=2,'lat'=4,'lev'=2,'sub'=2] {'lev','sub'}, dimensions={0} | all-to-all | bytes 17825792 | tf_op jit(solution)/shard_map/all_to_all | solution.py:64
  702.4 9.8 copy.61
  712.2 12.8 %copy.62 = bf16[34,4,32,2,512]{4,0,3,2,1:T(8,128)(2,1)} copy(bf16[34,4,32,2,512]{4,2,3,0,1:T(8,128)(2,1)} %bitcast.58) | data formatting | bytes 17825792 | tf_op jit(solution)/shard_map/all_to_all | solution.py:64
  725.0 33.8 %fusion.11 = bf16[128,34,2,512]{3,1,2,0:T(8,128)(2,1)} fusion(bf16[34,128,2,512]{3,0,2,1:T(8,128)(2,1)} %bitcast.55, bf16[128,512,512]{2,1,0:T(8,128)(2,1)} %all-gather.2.cloned.1.call-done), kind=kOutput, calls=%fused_computation.18 | convolution fusion | flops 4567859200 | bytes 84934656 | tf_op jit(solution)/shard_map/sxn,lscn->lxsc/dot_general | solution.py:65
  758.8 17.4 %copy.63 = bf16[34,512,256]{2,0,1:T(8,128)(2,1)} copy(bf16[34,512,256]{1,0,2:T(8,128)(2,1)} %bitcast.56) | data formatting | bytes 17825792 | tf_op jit(solution)/shard_map/reshape | solution.py:68
  776.2 6.2 all-to-all-start.3
  782.4 7.3 copy.66
  789.7 6.1 mul.115
  795.8 0.1 broadcast_in_dim.32
  795.9 0.2 mul.116
  796.1 214.2 %all-to-all-done.3 = bf16[34,512,256]{2,0,1:T(8,128)(2,1)} async-done(((bf16[34,512,256]{2,0,1:T(8,128)(2,1)}), bf16[34,512,256]{2,0,1:T(8,128)(2,1)}, u32[]{:S(2)}, u32[]{:S(2)}) %all-to-all-start.3) | async-done | bytes 8912928 | tf_op jit(solution)/shard_map/all_to_all | solution.py:69
  1010.3 12.9 %copy.65 = bf16[34,128,4,256]{3,2,1,0:T(4,128)(2,1)} copy(bf16[34,128,4,256]{3,0,1,2:T(8,128)(2,1)} %bitcast.21) | data formatting | bytes 17825792 | tf_op jit(solution)/shard_map/all_to_all | solution.py:69
  1023.2 9.9 copy.73
  1033.1 0.0 copy-start.1
  1033.1 15.6 %convolution_convert_fusion = bf16[4352,1024]{1,0:T(8,128)(2,1)} fusion(bf16[4352,1024]{1,0:T(8,128)(2,1)} %bitcast.60, f32[1024,1024]{0,1:T(8,128)} %mul.115, f32[1024]{0:T(1024)S(1)} %mul.116), kind=kOutput, calls=%fused_computation.15 | convolution fusion | flops 9133359104 | bytes 22024192 | tf_op jit(solution)/shard_map/dot_general | solution.py:70
  1048.7 0.0 copy-done.1
  (1 shorter events, 0.0 us)
Async XLA Ops:
  6.5 565.0 %copy-start = (bf16[32,136,136]{2,1,0:T(8,128)(2,1)S(1)}, bf16[32,136,136]{2,1,0:T(8,128)(2,1)}, u32[]{:S(2)}) copy-start(bf16[32,136,136]{2,1,0:T(8,128)(2,1)} %param.8) | copy-start | bytes 3551236
  6.5 0.8 copy-start.3
  6.5 397.8 %all-gather.2.cloned.1.call-start = ((), (), s32[]{:S(2)}) async-start(), calls=%async_computation.4 | async-start | bytes 83886080 | tf_op jit(solution)/shard_map/all_gather | solution.py:49
  31.5 13.7 %copy-start.2 = (bf16[1024,1024]{0,1:T(8,128)(2,1)S(1)}, bf16[1024,1024]{0,1:T(8,128)(2,1)}, u32[]{:S(2)}) copy-start(bf16[1024,1024]{0,1:T(8,128)(2,1)} %convert_element_type.68) | copy-start | bytes 6291460
  448.6 104.7 %all-to-all-start.1 = ((bf16[34,128,2,512]{3,2,0,1:T(2,128)(2,1)}), bf16[34,128,2,512]{3,2,0,1:T(2,128)(2,1)}, u32[]{:S(2)}, u32[]{:S(2)}) async-start(bf16[34,128,2,512]{3,2,0,1:T(2,128)(2,1)} %copy.56), calls=%async_computation.1 | async-start | bytes 17825792 | tf_op jit(solution)/shard_map/all_to_all | solution.py:55
  776.2 234.1 %all-to-all-start.3 = ((bf16[34,512,256]{2,0,1:T(8,128)(2,1)}), bf16[34,512,256]{2,0,1:T(8,128)(2,1)}, u32[]{:S(2)}, u32[]{:S(2)}) async-start(bf16[34,512,256]{2,0,1:T(8,128)(2,1)} %copy.63), calls=%async_computation.3 | async-start | bytes 20971520 | tf_op jit(solution)/shard_map/all_to_all | solution.py:69
  1033.1 15.6 %copy-start.1 = (bf16[32,136,136]{2,1,0:T(8,128)(2,1)S(1)}, bf16[32,136,136]{2,1,0:T(8,128)(2,1)}, u32[]{:S(2)}) copy-start(bf16[32,136,136]{2,1,0:T(8,128)(2,1)} %param.8) | copy-start | bytes 3551236
Sparse Core Ops, SparseCore 0:
  8.9 395.4 all-gather.1
where the time goes:
time: 1060 us
  waiting for transfers between devices  387 us (37%)
  blocking collectives  337 us (32%)
  local copies, waits for them, and re-layouts  172 us (16%)
  matrix products  108 us (10%)
  other arithmetic  26.4 us (2%)
  between operations  13.7 us (1%)
  starting transfers between devices  12.1 us (1%)
    all_to_all x1, blocking collectives, shards(): lax.all_to_all(spectral, 'lat', split_axis=2, concat_axis=1, tiled=True)  235 us
    all_to_all x1, waiting for transfers between devices, shards(): lax.all_to_all(synthesized, 'lat', split_axis=1, concat_axis=2, tiled=True)  214 us
    all_to_all x1, blocking collectives, shards(): lax.all_to_all(solved, ('lev', 'sub'), split_axis=0, concat_axis=1, tiled...  103 us
    all_to_all x1, waiting for transfers between devices, shards(): lax.all_to_all(part_spec, ('lev', 'sub'), split_axis=1, concat_axis=0, ti...  98.6 us
    all_gather x1, waiting for transfers between devices, shards(): lax.all_gather(spherical_basis_table, ('lev', 'sub'), axis=0, tiled=True)  73 us
    dot_general x1, matrix products, shards(): jnp.einsum('sxn,lscn->lxsc', gathered, returned, preferred_element_type=j...  33.8 us
    dot_general x1, matrix products, shards(): jnp.einsum('lxsc,sxn->lscn', by_slot, gathered, preferred_element_type=jn...  30.4 us
    reshape x2, local copies, waits for them, and re-layouts, shards(): by_slot = banded.reshape(layer_group_span, lat_total, owner_slots, 2)  24.9 us
  transfers between devices with their start and end apart: 3, of which 3 were waited for; matrix products, arithmetic and copies ran while one was open for 10% of the time, Pallas kernels for 0%

commit v1 on v0

--- a/solution.py
+++ b/solution.py
@@ -3,6 +3,20 @@
 import jax.numpy as jnp
 from jax import lax
 from jax.sharding import PartitionSpec as P
+
+
+def results_wrap(xx):
+    upper, spare = (lax.axis_size("lat"), lax.axis_index("lat"))
+    f_now = xx.shape[2] // upper
+    latest = jnp.roll(xx, -spare * f_now, axis=2)
+    slots = [lax.slice_in_dim(latest, 0, f_now, axis=2)]
+    for no in tuple(range(1, upper)):
+        left_arr = lax.slice_in_dim(latest, no * f_now, (no + 1) * f_now, axis=2)
+        w_next = lax.ppermute(left_arr, "lat", [(q, (q + no) % upper) for q in range(upper)])
+        slots.append(w_next)
+    tmp = jnp.concatenate(slots[::-1], axis=1)
+    side_arr = jnp.roll(tmp, (spare + 1) * slots[0].shape[1], axis=1)
+    return side_arr
 
 
 def raw_table(fourier_order_holder, lon_count):
@@ -45,7 +59,7 @@
     spectral = spectral.astype(jnp.bfloat16).reshape(
         layer_group_span, parallel_group_span, meridian_position
     )
-    banded = lax.all_to_all(spectral, "lat", split_axis=2, concat_axis=1, tiled=True)
+    banded = results_wrap(spectral)
     gathered = lax.all_gather(spherical_basis_table, ("lev", "sub"), axis=0, tiled=True)
     owner_slots = gathered.shape[0]
     by_slot = banded.reshape(layer_group_span, lat_total, owner_slots, 2)

time: 1060 us -> 1060 us (level)
  blocking collectives: 337 us -> 103 us
  waiting for transfers between devices: 387 us -> 592 us
  local copies, waits for them, and re-layouts: 172 us -> 185 us
    all_to_all x1 -> x0, blocking collectives: 235 us -> none  [shards(): lax.all_to_all(spectral, 'lat', split_axis=2, concat_axis=1, tiled=True)]
    ppermute x0 -> x3, waiting for transfers between devices: none -> 187 us  [results_wrap(): lax.ppermute(left_arr, 'lat', [(q, (q + no) % upper) for q in range(upper)])]
    reshape x3 -> x0, local copies, waits for them, and re-layouts: 40 us -> none  [the longest x2 24.9 us: shards(): by_slot = banded.reshape(layer_group_span, lat_total, owner_slots, 2)]
    unnamed x9 -> x20, local copies, waits for them, and re-layouts: 10 us -> 34.7 us
    dynamic_slice x0 -> x2, local copies, waits for them, and re-layouts: none -> 23.6 us  [results_wrap(): side_arr = jnp.roll(tmp, (spare + 1) * slots[0].shape[1], axis=1)]
    all_gather x1, waiting for transfers between devices: 73 us -> 91.6 us  [shards(): lax.all_gather(spherical_basis_table, ('lev', 'sub'), axis=0, tiled=True)]
  transfers between devices with their start and end apart: 3 -> 6, of which waited for: 3 -> 5; matrix products, arithmetic and copies ran while one was open for 10% -> 12% of each run, Pallas kernels for 0% -> 0%
where the time goes in v1:
time: 1060 us
  waiting for transfers between devices  592 us (56%)
  local copies, waits for them, and re-layouts  185 us (17%)
  matrix products  109 us (10%)
  blocking collectives  103 us (10%)
  other arithmetic  34.6 us (3%)
  starting transfers between devices  18.1 us (2%)
  between operations  13.7 us (1%)
    all_to_all x1, waiting for transfers between devices, shards(): lax.all_to_all(synthesized, 'lat', split_axis=1, concat_axis=2, tiled=True)  214 us
    ppermute x3, waiting for transfers between devices, results_wrap(): lax.ppermute(left_arr, 'lat', [(q, (q + no) % upper) for q in range(upper)])  187 us
    all_to_all x1, blocking collectives, shards(): lax.all_to_all(solved, ('lev', 'sub'), split_axis=0, concat_axis=1, tiled...  103 us
    all_to_all x1, waiting for transfers between devices, shards(): lax.all_to_all(part_spec, ('lev', 'sub'), split_axis=1, concat_axis=0, ti...  98.6 us
    all_gather x1, waiting for transfers between devices, shards(): lax.all_gather(spherical_basis_table, ('lev', 'sub'), axis=0, tiled=True)  91.6 us
    unnamed x20, local copies, waits for them, and re-layouts  34.7 us
    dot_general x1, matrix products, shards(): jnp.einsum('sxn,lscn->lxsc', gathered, returned, preferred_element_type=j...  33.8 us
    dot_general x1, matrix products, shards(): jnp.einsum('lxsc,sxn->lscn', by_slot, gathered, preferred_element_type=jn...  30.4 us
  transfers between devices with their start and end apart: 6, of which 5 were waited for; matrix products, arithmetic and copies ran while one was open for 12% of the time, Pallas kernels for 0%

profile of v1, /device:TPU:0, one launch (start us, length us, event | category | flops | bytes accessed | tf_op | source)
XLA Modules:
  0.0 1055.2 jit_solution(5182452712426769105)
XLA Ops:
  6.5 0.0 copy-start
  6.5 0.0 copy-start.5
  6.5 0.0 all-gather.2.cloned.1.call-start
  6.5 0.7 all-gather.2.cloned.1.call-update
  7.3 0.1 copy-done.5
  7.4 8.2 fusion.26
  15.6 4.4 maximum_multiply_fusion
  20.0 7.0 copy.36
  27.0 4.6 convert_element_type.68
  31.6 0.0 copy-start.4
  31.6 16.7 %fusion.5 = bf16[34,128,1024]{2,1,0:T(8,128)(2,1)} fusion(bf16[34,128,1024]{2,1,0:T(8,128)(2,1)} %param.5, bf16[34,128,1024]{2,1,0:T(8,128)(2,1)} %param.6), kind=kLoop, calls=%fused_computation.10 | loop fusion | flops 53477376 | bytes 26738688 | tf_op jit(solution)/shard_map/convert_element_type | solution.py:49
  48.3 0.0 copy-done.4
  48.3 13.4 %convolution_convert_fusion.1 = bf16[4352,1024]{1,0:T(8,128)(2,1)S(1)} fusion(bf16[4352,1024]{1,0:T(8,128)(2,1)} %bitcast.59, bf16[1024,1024]{0,1:T(8,128)(2,1)S(1)} %copy-done.4), kind=kOutput, calls=%fused_computation.18 | convolution fusion | flops 9131261952 | bytes 19922944 | tf_op jit(solution)/shard_map/dot_general | solution.py:54
  61.7 5.2 fusion.8
  66.9 0.0 copy-start.2
  66.9 3.6 copy-done.2
  70.4 3.1 fusion.28
  73.5 5.2 collective-permute-start
  78.7 0.0 collective-permute-start.1
  78.7 1.0 collective-permute-start.2
  79.7 0.0 copy-start.3
  79.7 48.2 %collective-permute-done = bf16[34,128,256]{2,1,0:T(8,128)(2,1)} collective-permute-done((bf16[34,128,256]{2,1,0:T(8,128)(2,1)}, bf16[34,128,256]{2,1,0:T(8,128)(2,1)}, u32[]{:S(2)}, u32[]{:S(2)}) %collective-permute-start) | collective-permute-done | bytes 2228256 | tf_op jit(solution)/shard_map/ppermute | solution.py:15
  127.9 3.3 constant_dynamic-update-slice_fusion.5
  131.2 138.4 %collective-permute-done.1 = bf16[34,128,256]{2,1,0:T(8,128)(2,1)} collective-permute-done((bf16[34,128,256]{2,1,0:T(8,128)(2,1)}, bf16[34,128,256]{2,1,0:T(8,128)(2,1)}, u32[]{:S(2)}, u32[]{:S(2)}) %collective-permute-start.1) | collective-permute-done | bytes 2228256 | tf_op jit(solution)/shard_map/ppermute | solution.py:15
  269.6 3.2 constant_dynamic-update-slice_fusion.4
  272.9 0.0 collective-permute-done.2
  272.9 3.3 constant_dynamic-update-slice_fusion.3
  276.1 0.0 copy-done.3
  276.1 1.7 slice_dynamic-update-slice_fusion
  277.8 3.2 constant_dynamic-update-slice_fusion.2
  281.0 3.2 constant_dynamic-update-slice_fusion.1
  284.2 3.2 constant_dynamic-update-slice_fusion
  287.5 1.7 slice_dynamic-update-slice_fusion.1
  289.1 8.1 constant_dynamic-slice_fusion
  297.2 15.5 %copy.37 = bf16[34,512,256]{1,0,2:T(8,128)(2,1)} copy(bf16[34,512,256]{2,1,0:T(8,128)(2,1)} %constant_dynamic-slice_fusion) | data formatting | bytes 17825792 | tf_op jit(solution)/shard_map/jit(_roll_dynamic)/dynamic_slice | solution.py:18
  312.8 91.6 %all-gather.2.cloned.1.call-done = bf16[128,512,512]{2,1,0:T(8,128)(2,1)} async-done(((bf16[32,512,512]{2,1,0:T(8,128)(2,1)}), bf16[128,512,512]{2,1,0:T(8,128)(2,1)}) %all-gather.2.cloned.1.call-update) | async-done | bytes 67108880 | tf_op jit(solution)/shard_map/all_gather | solution.py:63
  404.4 30.4 %convert_bitcast_fusion = bf16[34,128,2,512]{3,0,2,1:T(8,128)(2,1)} fusion(bf16[34,512,128,2]{1,0,3,2:T(8,128)(2,1)} %bitcast.50, bf16[128,512,512]{2,1,0:T(8,128)(2,1)} %all-gather.2.cloned.1.call-done), kind=kOutput, calls=%fused_computation.16 | convolution fusion | flops 4567859200 | bytes 84934656 | tf_op jit(solution)/shard_map/lxsc,sxn->lscn/dot_general | solution.py:66
  434.8 13.8 %copy.38 = bf16[34,128,2,512]{3,2,0,1:T(2,128)(2,1)} copy(bf16[34,128,2,512]{3,0,2,1:T(8,128)(2,1)} %convert_bitcast_fusion) | data formatting | bytes 17825792 | tf_op jit(solution)/shard_map/convert_element_type | solution.py:68
  448.6 5.7 all-to-all-start
  454.3 0.1 dynamic_slice.11
  454.4 0.1 iota_compare_fusion
  454.5 98.6 %all-to-all-done = bf16[34,128,2,512]{3,2,0,1:T(2,128)(2,1)} async-done(((bf16[34,128,2,512]{3,2,0,1:T(2,128)(2,1)}), bf16[34,128,2,512]{3,2,0,1:T(2,128)(2,1)}, u32[]{:S(2)}, u32[]{:S(2)}) %all-to-all-start) | async-done | bytes 8912928 | tf_op jit(solution)/shard_map/all_to_all | solution.py:69
  553.1 9.5 copy.39
  562.6 8.8 copy.40
  571.4 0.0 copy-done
  571.4 16.3 %fusion.15 = bf16[136,32,2,512]{3,0,2,1:T(8,128)(2,1)S(1)} fusion(bf16[136,32,2,512]{3,1,2,0:T(8,128)(2,1)} %bitcast.58, pred[32,512]{1,0:T(8,128)(4,1)S(1)} %iota_compare_fusion, bf16[32,136,136]{2,1,0:T(8,128)(2,1)S(1)} %copy-done), kind=kOutput, calls=%fused_computation.22 | convolution fusion | flops 1221066752 | bytes 19025920 | tf_op jit(solution)/shard_map/skl,lscn->kscn/dot_general | solution.py:70
  587.7 11.6 %copy.42 = bf16[136,32,2,512]{3,2,1,0:T(2,128)(2,1)S(1)} copy(bf16[136,32,2,512]{3,0,2,1:T(8,128)(2,1)S(1)} %fusion.15) | data formatting | bytes 17825792 | tf_op jit(solution)/shard_map/convert_element_type | solution.py:77
  599.3 102.7 %all_to_all.51 = bf16[136,32,2,512]{3,2,1,0:T(2,128)(2,1)} all-to-all(bf16[136,32,2,512]{3,2,1,0:T(2,128)(2,1)S(1)} %copy.42), channel_id=1, replica_groups=mesh['members'=2,'lat'=4,'lev'=2,'sub'=2] {'lev','sub'}, dimensions={0} | all-to-all | bytes 17825792 | tf_op jit(solution)/shard_map/all_to_all | solution.py:78
  702.0 9.8 copy.43
  711.7 12.8 %copy.44 = bf16[34,4,32,2,512]{4,0,3,2,1:T(8,128)(2,1)} copy(bf16[34,4,32,2,512]{4,2,3,0,1:T(8,128)(2,1)} %bitcast.54) | data formatting | bytes 17825792 | tf_op jit(solution)/shard_map/all_to_all | solution.py:78
  724.5 33.8 %fusion.12 = bf16[128,34,2,512]{3,1,2,0:T(8,128)(2,1)} fusion(bf16[34,128,2,512]{3,0,2,1:T(8,128)(2,1)} %bitcast.51, bf16[128,512,512]{2,1,0:T(8,128)(2,1)} %all-gather.2.cloned.1.call-done), kind=kOutput, calls=%fused_computation.21 | convolution fusion | flops 4567859200 | bytes 84934656 | tf_op jit(solution)/shard_map/sxn,lscn->lxsc/dot_general | solution.py:79
  758.3 17.4 %copy.45 = bf16[34,512,256]{2,0,1:T(8,128)(2,1)} copy(bf16[34,512,256]{1,0,2:T(8,128)(2,1)} %bitcast.52) | data formatting | bytes 17825792 | tf_op jit(solution)/shard_map/reshape | solution.py:82
  775.7 6.1 all-to-all-start.2
  781.8 7.3 copy.48
  789.1 6.1 mul.123
  795.2 0.1 broadcast_in_dim.32
  795.4 0.2 mul.124
  795.5 214.3 %all-to-all-done.2 = bf16[34,512,256]{2,0,1:T(8,128)(2,1)} async-done(((bf16[34,512,256]{2,0,1:T(8,128)(2,1)}), bf16[34,512,256]{2,0,1:T(8,128)(2,1)}, u32[]{:S(2)}, u32[]{:S(2)}) %all-to-all-start.2) | async-done | bytes 8912928 | tf_op jit(solution)/shard_map/all_to_all | solution.py:83
  1009.8 12.9 %copy.47 = bf16[34,128,4,256]{3,2,1,0:T(4,128)(2,1)} copy(bf16[34,128,4,256]{3,0,1,2:T(8,128)(2,1)} %bitcast.19) | data formatting | bytes 17825792 | tf_op jit(solution)/shard_map/all_to_all | solution.py:83
  1022.7 9.9 copy.52
  1032.6 0.0 copy-start.1
  1032.6 15.5 %convolution_convert_fusion = bf16[4352,1024]{1,0:T(8,128)(2,1)} fusion(bf16[4352,1024]{1,0:T(8,128)(2,1)} %bitcast.57, f32[1024,1024]{0,1:T(8,128)} %mul.123, f32[1024]{0:T(1024)S(1)} %mul.124), kind=kOutput, calls=%fused_computation.17 | convolution fusion | flops 9133359104 | bytes 22024192 | tf_op jit(solution)/shard_map/dot_general | solution.py:84
  1048.2 0.0 copy-done.1
  (1 shorter events, 0.0 us)
Async XLA Ops:
  6.5 564.9 %copy-start = (bf16[32,136,136]{2,1,0:T(8,128)(2,1)S(1)}, bf16[32,136,136]{2,1,0:T(8,128)(2,1)}, u32[]{:S(2)}) copy-start(bf16[32,136,136]{2,1,0:T(8,128)(2,1)} %param.8) | copy-start | bytes 3551236
  6.5 0.8 copy-start.5
  6.5 397.8 %all-gather.2.cloned.1.call-start = ((), (), s32[]{:S(2)}) async-start(), calls=%async_computation.3 | async-start | bytes 83886080 | tf_op jit(solution)/shard_map/all_gather | solution.py:63
  31.6 16.7 %copy-start.4 = (bf16[1024,1024]{0,1:T(8,128)(2,1)S(1)}, bf16[1024,1024]{0,1:T(8,128)(2,1)}, u32[]{:S(2)}) copy-start(bf16[1024,1024]{0,1:T(8,128)(2,1)} %convert_element_type.68) | copy-start | bytes 6291460
  66.9 3.6 copy-start.2
  73.5 54.4 %collective-permute-start = (bf16[34,128,256]{2,1,0:T(8,128)(2,1)}, bf16[34,128,256]{2,1,0:T(8,128)(2,1)}, u32[]{:S(2)}, u32[]{:S(2)}) collective-permute-start(bf16[34,128,256]{2,1,0:T(8,128)(2,1)} %get-tuple-element.7), channel_id=1, source_target_pairs={{0,12},{4,0},{8,4},{12,8},{1,13},{5,1},{9,5},{13,9},{2,14},{6,2},{... | collective-permute-start | bytes 6684680 | tf_op jit(solution)/shard_map/ppermute | solution.py:15
  78.7 190.9 %collective-permute-start.1 = (bf16[34,128,256]{2,1,0:T(8,128)(2,1)}, bf16[34,128,256]{2,1,0:T(8,128)(2,1)}, u32[]{:S(2)}, u32[]{:S(2)}) collective-permute-start(bf16[34,128,256]{2,1,0:T(8,128)(2,1)} %get-tuple-element.6), channel_id=1, source_target_pairs={{0,8},{4,12},{8,0},{12,4},{1,9},{5,13},{9,1},{13,5},{2,10},{6,14},... | collective-permute-start | bytes 6684680 | tf_op jit(solution)/shard_map/ppermute | solution.py:15
  78.7 194.2 %collective-permute-start.2 = (bf16[34,128,256]{2,1,0:T(8,128)(2,1)}, bf16[34,128,256]{2,1,0:T(8,128)(2,1)}, u32[]{:S(2)}, u32[]{:S(2)}) collective-permute-start(bf16[34,128,256]{2,1,0:T(8,128)(2,1)} %get-tuple-element.5), channel_id=1, source_target_pairs={{0,4},{4,8},{8,12},{12,0},{1,5},{5,9},{9,13},{13,1},{2,6},{6,10},{... | collective-permute-start | bytes 6684680 | tf_op jit(solution)/shard_map/ppermute | solution.py:15
  79.7 196.4 %copy-start.3 = (bf16[34,128,1024]{2,1,0:T(8,128)(2,1)S(1)}, bf16[34,128,1024]{2,1,0:T(8,128)(2,1)}, u32[]{:S(2)}) copy-start(bf16[34,128,1024]{2,1,0:T(8,128)(2,1)} %copy-done.2) | copy-start | bytes 26738692
  448.6 104.5 %all-to-all-start = ((bf16[34,128,2,512]{3,2,0,1:T(2,128)(2,1)}), bf16[34,128,2,512]{3,2,0,1:T(2,128)(2,1)}, u32[]{:S(2)}, u32[]{:S(2)}) async-start(bf16[34,128,2,512]{3,2,0,1:T(2,128)(2,1)} %copy.38), calls=%async_computation | async-start | bytes 17825792 | tf_op jit(solution)/shard_map/all_to_all | solution.py:69
  775.7 234.1 %all-to-all-start.2 = ((bf16[34,512,256]{2,0,1:T(8,128)(2,1)}), bf16[34,512,256]{2,0,1:T(8,128)(2,1)}, u32[]{:S(2)}, u32[]{:S(2)}) async-start(bf16[34,512,256]{2,0,1:T(8,128)(2,1)} %copy.45), calls=%async_computation.2 | async-start | bytes 20971520 | tf_op jit(solution)/shard_map/all_to_all | solution.py:83
  1032.6 15.6 %copy-start.1 = (bf16[32,136,136]{2,1,0:T(8,128)(2,1)S(1)}, bf16[32,136,136]{2,1,0:T(8,128)(2,1)}, u32[]{:S(2)}) copy-start(bf16[32,136,136]{2,1,0:T(8,128)(2,1)} %param.8) | copy-start | bytes 3551236
Sparse Core Ops, SparseCore 0:
  8.9 395.4 all-gather.1
